TPU v7x, 32 devices: a whole 2x2x4 slice. The times are simulated.
32 devices in a mesh: band: 8 (over z, y), mode: 4 (over x, core).
Axes of the slice: x: 2, y: 2, z: 4, core: 2. Of those that a mesh axis runs over, the one named last changes fastest.
Arguments:
- velocity: bfloat16 [1, 8192, 1024], P(None, ('band', 'mode')), may hold values from -6 to 6
- radiation_modes: bfloat16 [8192, 1024], P('band', 'mode'), may hold values from -0.125 to 0.125
- resistance: float32 [8, 1024, 1024], P('band', None, 'mode'), as said below
- mode_ranks: int32 [8], P('band'), may hold values from 128 to 1024, as said below
- freq_table: int32 [512], replicated, may hold values from 0 to 511, each once
Outputs:
- adjoint_force: bfloat16 [1, 8192, 1024], P(None, ('band', 'mode'))
Inputs may be any that keep to these rules, and one draw needn't show every extreme that they name: `resistance`: each band's matrix is symmetric. `mode_ranks`: the ranks never fall with the band index; the first band keeps 1024 // 8 modes and the last 1024.
All inputs are finite; a program needn't handle non-finite values.
Results may differ from a plain program's by a relative error of at most 0.015.
Values may be sent and summed in bfloat16 or wider, within the bound.
A program may use at most 64 MiB of HBM per device.

v0:
```python
import math
import jax
import jax.numpy as jnp
from jax import lax
from jax.sharding import PartitionSpec as P


def make_table(freq_table, step_count):
    times = jnp.arange(step_count, dtype=jnp.int32)
    phases = times[:, None] * freq_table[None, :] % step_count
    angles = phases.astype(jnp.float32) * (2.0 * math.pi / step_count)
    norming = 1.0 / math.sqrt(step_count)
    table = jnp.stack([jnp.cos(angles), -jnp.sin(angles)], axis=1) * norming
    return table.astype(jnp.bfloat16)


def add_sources(received):
    return jnp.sum(received, axis=0)


def per_device(velocity, radiation_modes, resistance, mode_ranks, freq_table):
    step_count = velocity.shape[2]
    mode_cols = radiation_modes.shape[1]
    dft_table = make_table(freq_table, step_count)
    spectra = jnp.einsum(
        "wpt,tcf->wpcf", velocity, dft_table, preferred_element_type=jnp.float32
    ).astype(jnp.bfloat16)
    partial_value = jnp.einsum(
        "wpcf,pr->wrcf",
        lax.all_gather(spectra, "mode", axis=1, tiled=True),
        radiation_modes,
        preferred_element_type=jnp.float32,
    )
    coefficients = add_sources(
        lax.all_to_all(
            partial_value[None].astype(jnp.bfloat16),
            "band",
            split_axis=4,
            concat_axis=0,
            tiled=True,
        ).astype(jnp.float32)
    )
    offset = lax.axis_index("mode") * mode_cols
    rank_here = mode_ranks[0]
    kept_mask = (offset + jnp.arange(mode_cols, dtype=jnp.int32) < rank_here).astype(jnp.float32)
    kept_mask = kept_mask[None, :, None, None]
    coefficients = coefficients * kept_mask
    matrix = resistance[0]
    partial_terms = jnp.einsum(
        "ij,wjcf->wicf", matrix, coefficients, precision=lax.Precision.HIGHEST
    )
    forcing = lax.psum_scatter(
        partial_terms.astype(jnp.bfloat16), "mode", scatter_dimension=1, tiled=True
    ).astype(jnp.float32)
    forcing = (2.0 * forcing * kept_mask).astype(jnp.bfloat16)
    collected = lax.all_gather(forcing, "mode", axis=1, tiled=True)
    collected = lax.all_gather(collected, "band", axis=3, tiled=True)
    own_basis = lax.all_to_all(radiation_modes, "mode", split_axis=0, concat_axis=1, tiled=True)
    surface_force = jnp.einsum(
        "pr,wrcf->wpcf", own_basis, collected, preferred_element_type=jnp.float32
    ).astype(jnp.bfloat16)
    history = jnp.einsum(
        "wpcf,tcf->wpt", surface_force, dft_table, preferred_element_type=jnp.float32
    )
    return history.astype(jnp.bfloat16)


def solution(mesh):
    placed = (
        P(None, ("band", "mode"), None),
        P("band", "mode"),
        P("band", None, "mode"),
        P("band"),
        P(),
    )
    return jax.shard_map(
        per_device,
        mesh=mesh,
        in_specs=placed,
        out_specs=P(None, ("band", "mode"), None),
        check_vma=False,
    )
```

profile of v0, /device:TPU:0, one launch (start us, length us, event | category | flops | bytes accessed | tf_op | source)
XLA Modules:
  0.0 158.5 jit_solution(3879735066893673971)
XLA Ops:
  6.5 9.1 %fusion.21 = (f32[1024,1,512]{0,2,1:T(8,128)S(1)}, f32[1024,1,512]{0,2,1:T(8,128)S(1)}) fusion(s32[512]{0:T(512)} %param.9), kind=kLoop, calls=%fused_computation.27 | loop fusion | flops 7864320 | bytes 4196352 | tf_op jit(solution)/shard_map/cos | solution.py:13
  15.7 1.3 copy-done.1
  17.0 0.6 copy-done.2
  17.7 1.6 fusion.13
  19.2 0.0 all-gather.6.cloned.1.call-update
  19.2 25.7 %all-gather.6.cloned.1.call-done = bf16[1024,2,512]{0,2,1:T(8,128)(2,1)} async-done(((bf16[256,2,512]{0,2,1:T(8,128)(2,1)}), bf16[1024,2,512]{0,2,1:T(8,128)(2,1)}) %all-gather.6.cloned.1.call-update) | async-done | bytes 2097168 | tf_op jit(solution)/shard_map/all_gather | solution.py:30
  44.9 2.3 %fusion.14 = bf16[1,1,256,2,512]{2,4,3,1,0:T(8,128)(2,1)S(1)} fusion(bf16[1024,2,512]{0,2,1:T(8,128)(2,1)} %all-gather.6.cloned.1.call-done, bf16[1024,256]{1,0:T(8,128)(2,1)S(1)} %copy-done.3), kind=kOutput, calls=%fused_computation.20 | convolution fusion | flops 537133056 | bytes 3145728 | tf_op jit(solution)/shard_map/wpcf,pr->wrcf/dot_general | solution.py:28
  47.2 1.3 copy.16
  48.6 5.5 %all-to-all-start = ((bf16[1,1,256,2,512]{2,3,1,0,4:T(2,128)(2,1)}), bf16[1,1,256,2,512]{2,3,1,0,4:T(2,128)(2,1)S(1)}, u32[]{:S(2)}, u32[]{:S(2)}) async-start(bf16[1,1,256,2,512]{2,3,1,0,4:T(2,128)(2,1)} %copy.16), calls=%async_computation | async-start | bytes 1048576 | tf_op jit(solution)/shard_map/all_to_all | solution.py:35
  54.1 0.2 reduce-scatter.2.cloned.1.call-start
  55.0 14.0 %all-to-all-done = bf16[1,1,256,2,512]{2,3,1,0,4:T(2,128)(2,1)S(1)} async-done(((bf16[1,1,256,2,512]{2,3,1,0,4:T(2,128)(2,1)}), bf16[1,1,256,2,512]{2,3,1,0,4:T(2,128)(2,1)S(1)}, u32[]{:S(2)}, u32[]{:S(2)}) %all-to-all-start) | async-done | bytes 524320 | tf_op jit(solution)/shard_map/all_to_all | solution.py:35
  69.0 0.5 convert_reduce_fusion
  69.5 1.9 %fusion.19 = bf16[1,1024,2,64]{1,3,2,0:T(8,128)(2,1)} fusion(f32[1,1024,256]{2,1,0:T(8,128)S(1)} %copy-done, f32[256,2,64]{0,1,2:T(2,128)S(1)} %convert_reduce_fusion, f32[256]{0:T(256)S(1)} %fusion.30), kind=kOutput, calls=%fused_computation.24 | convolution fusion | flops 402817024 | bytes 1442816 | tf_op jit(solution)/shard_map/ij,wjcf->wicf/dot_general | solution.py:49
  71.4 0.0 reduce-scatter.2.cloned.1.call-update
  71.4 0.0 all-gather.4.cloned.1.call-start
  71.5 18.3 %reduce-scatter.2.cloned.1.call-done = bf16[1,256,2,64]{1,3,2,0:T(8,128)(2,1)} async-done(((bf16[1,1024,2,64]{1,3,2,0:T(8,128)(2,1)}), bf16[1,256,2,64]{1,3,2,0:T(8,128)(2,1)}) %reduce-scatter.2.cloned.1.call-update) | async-done | bytes 65552 | tf_op jit(solution)/shard_map/reduce_scatter | solution.py:52
  89.7 0.9 multiply_convert_fusion
  90.6 6.2 %all_gather.10 = bf16[1,1024,2,64]{1,3,2,0:T(8,128)(2,1)} all-gather(bf16[1,256,2,64]{1,3,2,0:T(8,128)(2,1)S(1)} %multiply_convert_fusion), channel_id=1, replica_groups=mesh['band'=8,'mode'=4] {'mode'}, dimensions={1}, use_global_device_ids=true | all-gather | bytes 327680 | tf_op jit(solution)/shard_map/all_gather | solution.py:56
  96.8 0.0 all-gather.4.cloned.1.call-update
  96.8 11.2 %all_to_all.28 = bf16[4,256,256]{2,1,0:T(8,128)(2,1)S(1)} all-to-all(bf16[4,256,256]{2,1,0:T(8,128)(2,1)S(1)} %bitcast.57), channel_id=1, replica_groups=mesh['band'=8,'mode'=4] {'mode'}, dimensions={0} | all-to-all | bytes 1048576 | tf_op jit(solution)/shard_map/all_to_all | solution.py:58
  108.1 0.4 copy.18
  108.5 0.4 reshape.162
  108.8 37.2 %all-gather.4.cloned.1.call-done = bf16[1,1024,2,512]{1,3,2,0:T(8,128)(2,1)} async-done(((bf16[1,1024,2,64]{1,3,2,0:T(8,128)(2,1)}), bf16[1,1024,2,512]{1,3,2,0:T(8,128)(2,1)}) %all-gather.4.cloned.1.call-update) | async-done | bytes 2097168 | tf_op jit(solution)/shard_map/all_gather | solution.py:57
  146.1 5.9 %fusion.18 = bf16[1,256,1024]{2,1,0:T(8,128)(2,1)} fusion(bf16[256,1024,1]{1,0,2:T(8,128)(2,1)S(1)} %reshape.162, bf16[1,1024,2,512]{1,3,2,0:T(8,128)(2,1)} %all-gather.4.cloned.1.call-done, f32[1024,1,512]{0,2,1:T(8,128)} %copy-done.2, f32[1024,1,512]{0,2,1:T(8,128)} %copy-done.1), kind=kOutput, calls=%fused_computation.22 | convolution fusion | flops 1077411840 | bytes 7340032 | tf_op jit(solution)/shard_map/wpcf,tcf->wpt/dot_general | solution.py:62
  (11 shorter events, 0.0 us)
Async XLA Ops:
  6.5 62.9 %copy-start = (f32[1,1024,256]{2,1,0:T(8,128)S(1)}, f32[1,1024,256]{2,1,0:T(8,128)}, u32[]{:S(2)}) copy-start(f32[1,1024,256]{2,1,0:T(8,128)} %param.7) | copy-start | bytes 3145732
  6.5 11.1 %copy-start.4 = (bf16[1,256,1024]{2,1,0:T(8,128)(2,1)S(1)}, bf16[1,256,1024]{2,1,0:T(8,128)(2,1)}, u32[]{:S(2)}) copy-start(bf16[1,256,1024]{2,1,0:T(8,128)(2,1)} %param.5) | copy-start | bytes 1572868
  6.5 38.4 %all-gather.6.cloned.1.call-start = ((), (), s32[]{:S(2)}) async-start(), calls=%async_computation.5 | async-start | bytes 2621440 | tf_op jit(solution)/shard_map/all_gather | solution.py:30
  15.7 1.3 copy-start.1
  15.7 1.9 %copy-start.2 = (f32[1024,1,512]{0,2,1:T(8,128)}, f32[1024,1,512]{0,2,1:T(8,128)S(1)}, u32[]{:S(2)}) copy-start(f32[1024,1,512]{0,2,1:T(8,128)S(1)} %get-tuple-element.6) | copy-start | bytes 6291460
  17.7 27.3 %copy-start.3 = (bf16[1024,256]{1,0:T(8,128)(2,1)S(1)}, bf16[1024,256]{1,0:T(8,128)(2,1)}, u32[]{:S(2)}) copy-start(bf16[1024,256]{1,0:T(8,128)(2,1)} %param.6) | copy-start | bytes 1572868
  48.6 20.4 %all-to-all-start = ((bf16[1,1,256,2,512]{2,3,1,0,4:T(2,128)(2,1)}), bf16[1,1,256,2,512]{2,3,1,0,4:T(2,128)(2,1)S(1)}, u32[]{:S(2)}, u32[]{:S(2)}) async-start(bf16[1,1,256,2,512]{2,3,1,0,4:T(2,128)(2,1)} %copy.16), calls=%async_computation | async-start | bytes 1048576 | tf_op jit(solution)/shard_map/all_to_all | solution.py:35
  54.1 35.7 %reduce-scatter.2.cloned.1.call-start = ((), (), s32[]{:S(2)}) async-start(), calls=%async_computation.3 | async-start | bytes 327680 | tf_op jit(solution)/shard_map/reduce_scatter | solution.py:52
  71.4 74.7 %all-gather.4.cloned.1.call-start = ((), (), s32[]{:S(2)}) async-start(), calls=%async_computation.4 | async-start | bytes 2359296 | tf_op jit(solution)/shard_map/all_gather | solution.py:57
Sparse Core Ops, SparseCore 0:
  19.4 25.5 all-gather.5
  71.5 18.1 reduce-scatter.1
  97.0 49.0 all-gather.3
where the time goes:
time: 159 us
  waiting for transfers between devices  95.3 us (60%)
  blocking collectives  17.4 us (11%)
  between operations  13.8 us (9%)
  matrix products  11.7 us (7%)
  other arithmetic  10.5 us (7%)
  starting transfers between devices  5.78 us (4%)
  local copies, waits for them, and re-layouts  4.06 us (3%)
    all_gather x1, waiting for transfers between devices, per_device(): collected = lax.all_gather(collected, 'band', axis=3, tiled=True)  37.2 us
    all_gather x1, waiting for transfers between devices, per_device(): lax.all_gather(spectra, 'mode', axis=1, tiled=True)  25.7 us
    reduce_scatter x1, waiting for transfers between devices, per_device(): lax.psum_scatter(partial_terms.astype(jnp.bfloat16), 'mode', scatter_dime...  18.3 us
    all_to_all x1, waiting for transfers between devices, per_device(): lax.all_to_all(partial_value[None].astype(jnp.bfloat16), 'band', split_ax...  14 us
    all_to_all x1, blocking collectives, per_device(): lax.all_to_all(radiation_modes, 'mode', split_axis=0, concat_axis=1, tile...  11.2 us
    cos x1, other arithmetic, make_table(): table = jnp.stack([jnp.cos(angles), -jnp.sin(angles)], axis=1) * norming  9.14 us
    all_gather x1, blocking collectives, per_device(): collected = lax.all_gather(forcing, 'mode', axis=1, tiled=True)  6.23 us
    dot_general x1, matrix products, per_device(): jnp.einsum('wpcf,tcf->wpt', surface_force, dft_table, preferred_element_t...  5.95 us
  transfers between devices with their start and end apart: 4, of which 4 were waited for; matrix products, arithmetic and copies ran while one was open for 0% of the time, Pallas kernels for 0%

commit v1 on v0

--- a/solution.py
+++ b/solution.py
@@ -54,7 +54,7 @@
     ).astype(jnp.float32)
     forcing = (2.0 * forcing * kept_mask).astype(jnp.bfloat16)
     collected = lax.all_gather(forcing, "mode", axis=1, tiled=True)
-    collected = lax.all_gather(collected, "band", axis=3, tiled=True)
+    collected = jnp.concatenate(lax.all_gather(collected, "band"), axis=3)
     own_basis = lax.all_to_all(radiation_modes, "mode", split_axis=0, concat_axis=1, tiled=True)
     surface_force = jnp.einsum(
         "pr,wrcf->wpcf", own_basis, collected, preferred_element_type=jnp.float32

time: 159 us -> 160 us (level)
  local copies, waits for them, and re-layouts: 4.06 us -> 6.73 us
    all_gather x0 -> x1, local copies, waits for them, and re-layouts: none -> 1.85 us  [per_device(): collected = jnp.concatenate(lax.all_gather(collected, 'band'), axis=3)]
  transfers between devices with their start and end apart: 4 -> 4, of which waited for: 4 -> 4; matrix products, arithmetic and copies ran while one was open for 0% -> 1% of each run, Pallas kernels for 0% -> 0%
where the time goes in v1:
time: 160 us
  waiting for transfers between devices  94.5 us (59%)
  blocking collectives  17.4 us (11%)
  between operations  13.8 us (9%)
  matrix products  11.2 us (7%)
  other arithmetic  10.5 us (7%)
  local copies, waits for them, and re-layouts  6.73 us (4%)
  starting transfers between devices  5.78 us (4%)
    all_gather x1, waiting for transfers between devices, per_device(): collected = jnp.concatenate(lax.all_gather(collected, 'band'), axis=3)  36.4 us
    all_gather x1, waiting for transfers between devices, per_device(): lax.all_gather(spectra, 'mode', axis=1, tiled=True)  25.7 us
    reduce_scatter x1, waiting for transfers between devices, per_device(): lax.psum_scatter(partial_terms.astype(jnp.bfloat16), 'mode', scatter_dime...  18.3 us
    all_to_all x1, waiting for transfers between devices, per_device(): lax.all_to_all(partial_value[None].astype(jnp.bfloat16), 'band', split_ax...  14 us
    all_to_all x1, blocking collectives, per_device(): lax.all_to_all(radiation_modes, 'mode', split_axis=0, concat_axis=1, tile...  11.2 us
    cos x1, other arithmetic, make_table(): table = jnp.stack([jnp.cos(angles), -jnp.sin(angles)], axis=1) * norming  9.14 us
    all_gather x1, blocking collectives, per_device(): collected = lax.all_gather(forcing, 'mode', axis=1, tiled=True)  6.23 us
    all_to_all x1, starting transfers between devices, per_device(): lax.all_to_all(partial_value[None].astype(jnp.bfloat16), 'band', split_ax...  5.52 us
  transfers between devices with their start and end apart: 4, of which 4 were waited for; matrix products, arithmetic and copies ran while one was open for 1% of the time, Pallas kernels for 0%

profile of v1, /device:TPU:0, one launch (start us, length us, event | category | flops | bytes accessed | tf_op | source)
XLA Modules:
  0.0 159.9 jit_solution(7024196376949628525)
XLA Ops:
  6.5 9.1 %fusion.14 = (f32[1024,1,512]{0,2,1:T(8,128)S(1)}, f32[1024,1,512]{0,2,1:T(8,128)S(1)}) fusion(s32[512]{0:T(512)} %param.9), kind=kLoop, calls=%fused_computation.25 | loop fusion | flops 7864320 | bytes 4196352 | tf_op jit(solution)/shard_map/cos | solution.py:13
  15.7 1.3 copy-done.1
  17.0 0.6 copy-done.2
  17.7 1.6 fusion.8
  19.2 25.7 %all-gather.5.cloned.1.call-done = bf16[1024,2,512]{0,2,1:T(8,128)(2,1)} async-done(((bf16[256,2,512]{0,2,1:T(8,128)(2,1)}), bf16[1024,2,512]{0,2,1:T(8,128)(2,1)}) %all-gather.5.cloned.1.call-update) | async-done | bytes 2097168 | tf_op jit(solution)/shard_map/all_gather | solution.py:30
  44.9 2.3 %fusion.9 = bf16[1,1,256,2,512]{2,4,3,1,0:T(8,128)(2,1)S(1)} fusion(bf16[1024,2,512]{0,2,1:T(8,128)(2,1)} %all-gather.5.cloned.1.call-done, bf16[1024,256]{1,0:T(8,128)(2,1)S(1)} %copy-done.3), kind=kOutput, calls=%fused_computation.18 | convolution fusion | flops 537133056 | bytes 3145728 | tf_op jit(solution)/shard_map/wpcf,pr->wrcf/dot_general | solution.py:28
  47.2 1.3 copy.22
  48.6 5.5 %all-to-all-start = ((bf16[1,1,256,2,512]{2,3,1,0,4:T(2,128)(2,1)}), bf16[1,1,256,2,512]{2,3,1,0,4:T(2,128)(2,1)S(1)}, u32[]{:S(2)}, u32[]{:S(2)}) async-start(bf16[1,1,256,2,512]{2,3,1,0,4:T(2,128)(2,1)} %copy.22), calls=%async_computation | async-start | bytes 1048576 | tf_op jit(solution)/shard_map/all_to_all | solution.py:35
  54.1 0.2 reduce-scatter.2.cloned.1.call-start
  55.0 14.0 %all-to-all-done = bf16[1,1,256,2,512]{2,3,1,0,4:T(2,128)(2,1)S(1)} async-done(((bf16[1,1,256,2,512]{2,3,1,0,4:T(2,128)(2,1)}), bf16[1,1,256,2,512]{2,3,1,0,4:T(2,128)(2,1)S(1)}, u32[]{:S(2)}, u32[]{:S(2)}) %all-to-all-start) | async-done | bytes 524320 | tf_op jit(solution)/shard_map/all_to_all | solution.py:35
  69.0 0.5 convert_reduce_fusion
  69.5 1.9 %fusion.12 = bf16[1,1024,2,64]{1,3,2,0:T(8,128)(2,1)} fusion(f32[1,1024,256]{2,1,0:T(8,128)S(1)} %copy-done, f32[256,2,64]{0,1,2:T(2,128)S(1)} %convert_reduce_fusion, f32[256]{0:T(256)S(1)} %fusion.21), kind=kOutput, calls=%fused_computation.22 | convolution fusion | flops 402817024 | bytes 1442816 | tf_op jit(solution)/shard_map/ij,wjcf->wicf/dot_general | solution.py:49
  71.4 0.0 reduce-scatter.2.cloned.1.call-update
  71.4 0.0 all-gather.7.cloned.1.call-start
  71.5 18.3 %reduce-scatter.2.cloned.1.call-done = bf16[1,256,2,64]{1,3,2,0:T(8,128)(2,1)} async-done(((bf16[1,1024,2,64]{1,3,2,0:T(8,128)(2,1)}), bf16[1,256,2,64]{1,3,2,0:T(8,128)(2,1)}) %reduce-scatter.2.cloned.1.call-update) | async-done | bytes 65552 | tf_op jit(solution)/shard_map/reduce_scatter | solution.py:52
  89.7 0.9 multiply_convert_fusion
  90.6 6.2 %all_gather.13 = bf16[1,1024,2,64]{1,3,2,0:T(8,128)(2,1)} all-gather(bf16[1,256,2,64]{1,3,2,0:T(8,128)(2,1)S(1)} %multiply_convert_fusion), channel_id=1, replica_groups=mesh['band'=8,'mode'=4] {'mode'}, dimensions={1}, use_global_device_ids=true | all-gather | bytes 327680 | tf_op jit(solution)/shard_map/all_gather | solution.py:56
  96.8 0.0 all-gather.7.cloned.1.call-update
  96.8 11.2 %all_to_all.28 = bf16[4,256,256]{2,1,0:T(8,128)(2,1)S(1)} all-to-all(bf16[4,256,256]{2,1,0:T(8,128)(2,1)S(1)} %bitcast.55), channel_id=1, replica_groups=mesh['band'=8,'mode'=4] {'mode'}, dimensions={0} | all-to-all | bytes 1048576 | tf_op jit(solution)/shard_map/all_to_all | solution.py:58
  108.1 0.4 copy.25
  108.5 1.2 reshape.169
  109.7 36.4 %all-gather.7.cloned.1.call-done = bf16[8,1024,2,64]{1,3,2,0:T(8,128)(2,1)} async-done(((bf16[1,1024,2,64]{1,3,2,0:T(8,128)(2,1)}), bf16[8,1024,2,64]{1,3,2,0:T(8,128)(2,1)}) %all-gather.7.cloned.1.call-update) | async-done | bytes 2097168 | tf_op jit(solution)/shard_map/all_gather | solution.py:57
  146.1 1.8 %copy.24 = bf16[8,1024,2,64]{1,3,0,2:T(8,128)(2,1)S(1)} copy(bf16[8,1024,2,64]{1,3,2,0:T(8,128)(2,1)} %all-gather.7.cloned.1.call-done) | data formatting | bytes 4194304 | tf_op jit(solution)/shard_map/all_gather | solution.py:57
  147.9 5.5 %fusion.11 = bf16[1,256,1024]{2,1,0:T(8,128)(2,1)} fusion(bf16[1024,2,512]{0,2,1:T(8,128)(2,1)S(1)} %bitcast.53, bf16[256,1024,1]{1,0,2:T(8,128)(2,1)} %reshape.169, f32[1024,1,512]{0,2,1:T(8,128)} %copy-done.2, f32[1024,1,512]{0,2,1:T(8,128)} %copy-done.1), kind=kOutput, calls=%fused_computation.20 | convolution fusion | flops 1077411840 | bytes 7340032 | tf_op jit(solution)/shard_map/wpcf,tcf->wpt/dot_general | solution.py:62
  (12 shorter events, 0.0 us)
Async XLA Ops:
  6.5 62.9 %copy-start = (f32[1,1024,256]{2,1,0:T(8,128)S(1)}, f32[1,1024,256]{2,1,0:T(8,128)}, u32[]{:S(2)}) copy-start(f32[1,1024,256]{2,1,0:T(8,128)} %param.7) | copy-start | bytes 3145732
  6.5 11.1 %copy-start.4 = (bf16[1,256,1024]{2,1,0:T(8,128)(2,1)S(1)}, bf16[1,256,1024]{2,1,0:T(8,128)(2,1)}, u32[]{:S(2)}) copy-start(bf16[1,256,1024]{2,1,0:T(8,128)(2,1)} %param.5) | copy-start | bytes 1572868
  6.5 38.4 %all-gather.5.cloned.1.call-start = ((), (), s32[]{:S(2)}) async-start(), calls=%async_computation.4 | async-start | bytes 2621440 | tf_op jit(solution)/shard_map/all_gather | solution.py:30
  15.7 1.3 copy-start.1
  15.7 1.9 %copy-start.2 = (f32[1024,1,512]{0,2,1:T(8,128)}, f32[1024,1,512]{0,2,1:T(8,128)S(1)}, u32[]{:S(2)}) copy-start(f32[1024,1,512]{0,2,1:T(8,128)S(1)} %get-tuple-element.6) | copy-start | bytes 6291460
  17.7 27.3 %copy-start.3 = (bf16[1024,256]{1,0:T(8,128)(2,1)S(1)}, bf16[1024,256]{1,0:T(8,128)(2,1)}, u32[]{:S(2)}) copy-start(bf16[1024,256]{1,0:T(8,128)(2,1)} %param.6) | copy-start | bytes 1572868
  48.6 20.4 %all-to-all-start = ((bf16[1,1,256,2,512]{2,3,1,0,4:T(2,128)(2,1)}), bf16[1,1,256,2,512]{2,3,1,0,4:T(2,128)(2,1)S(1)}, u32[]{:S(2)}, u32[]{:S(2)}) async-start(bf16[1,1,256,2,512]{2,3,1,0,4:T(2,128)(2,1)} %copy.22), calls=%async_computation | async-start | bytes 1048576 | tf_op jit(solution)/shard_map/all_to_all | solution.py:35
  54.1 35.7 %reduce-scatter.2.cloned.1.call-start = ((), (), s32[]{:S(2)}) async-start(), calls=%async_computation.3 | async-start | bytes 327680 | tf_op jit(solution)/shard_map/reduce_scatter | solution.py:52
  71.4 74.7 %all-gather.7.cloned.1.call-start = ((), (), s32[]{:S(2)}) async-start(), calls=%async_computation.5 | async-start | bytes 2359296 | tf_op jit(solution)/shard_map/all_gather | solution.py:57
Sparse Core Ops, SparseCore 0:
  19.4 25.5 all-gather.4
  71.5 18.1 reduce-scatter.1
  97.0 49.0 all-gather.6
